TPU v7x, 32 devices: a whole 2x2x4 slice. The times are simulated.
32 devices in a mesh: lat: 8 (over z, y), rep: 4 (over x, core).
Axes of the slice: x: 2, y: 2, z: 4, core: 2. Of those that a mesh axis runs over, the one named last changes fastest.
Arguments:
- legendre_table: bfloat16 [1024, 4, 8, 1025], P('lat', 'rep'), may hold values from -0.1875 to 0.1875
- fourier: bfloat16 [2, 1024, 4, 8, 2, 24], P(None, 'lat', None, None, None, 'rep'), may hold values from -6 to 6
- pair_low: int32 [4, 8], replicated, may hold values from 0 to 511
Outputs:
- spectral: float32 [4, 8, 1025, 24], P(None, 'lat', None, 'rep')
Inputs may be any that keep to these rules, and one draw needn't show every extreme that they name: The pair slot holds the wavenumbers pair_low and 1023 - pair_low.
All inputs are finite; a program needn't handle non-finite values.
Results may differ from a plain program's by a relative error of at most 0.0031.
Values may be sent and summed in bfloat16 or wider, within the bound.
A program may use at most 64 MiB of HBM per device.

v0:
```python
import jax
import jax.numpy as jnp
from jax import lax
from jax.sharding import PartitionSpec as P

TRUNC = 1024


def selector(lows, width):
    column = jnp.arange(width, dtype=jnp.int32)
    split = (TRUNC - lows)[..., None]
    upper = column >= split
    offset = jnp.where(upper, column - split, column)
    index = 2 * upper.astype(jnp.int32) + offset % 2
    return index[..., None, :] == jnp.arange(4, dtype=jnp.int32)[:, None]


def combine(fourier):
    north = fourier[0].astype(jnp.float32)
    south = fourier[1].astype(jnp.float32)
    parts = [
        north[..., 0, :] + south[..., 0, :],
        north[..., 0, :] - south[..., 0, :],
        north[..., 1, :] + south[..., 1, :],
        north[..., 1, :] - south[..., 1, :],
    ]
    return jnp.stack(parts, axis=-2).astype(jnp.bfloat16)


def local_sums(table_blk, fourier_blk, lows_blk):
    combos = combine(fourier_blk)
    chosen = selector(lows_blk, table_blk.shape[3]).astype(jnp.bfloat16)
    masked = table_blk[:, :, :, None, :] * chosen[None]
    return jnp.einsum("ljoqc,ljoqf->jocf", masked, combos, preferred_element_type=jnp.float32)


def per_device(legendre_table, fourier, pair_low):
    quarter = legendre_table.shape[1]
    lows_blk = lax.dynamic_slice_in_dim(pair_low, lax.axis_index("rep") * quarter, quarter, 0)
    lows_own = lax.dynamic_slice_in_dim(lows_blk, lax.axis_index("lat"), 1, 1)
    table_blk = lax.all_to_all(legendre_table, "lat", split_axis=2, concat_axis=0, tiled=True)
    fourier_blk = lax.all_to_all(
        lax.all_to_all(fourier, "lat", split_axis=3, concat_axis=1, tiled=True),
        "rep",
        split_axis=2,
        concat_axis=5,
        tiled=True,
    )
    owned = local_sums(table_blk, fourier_blk, lows_own)
    spectral = lax.all_to_all(owned, "rep", split_axis=3, concat_axis=0, tiled=True)
    return spectral


def solution(mesh):
    return jax.shard_map(
        per_device,
        mesh=mesh,
        in_specs=(P("lat", "rep", None, None), P(None, "lat", None, None, None, "rep"), P()),
        out_specs=P(None, "lat", None, "rep"),
        check_vma=False,
    )
```

profile of v0, /device:TPU:0, one launch (start us, length us, event | category | flops | bytes accessed | tf_op | source)
XLA Modules:
  0.0 92.1 jit_solution(4450313428376648307)
XLA Ops:
  0.0 1.1 %copy.21 = bf16[2,128,4,8,2,6]{1,4,5,2,0,3:T(2,128)(2,1)S(1)} copy(bf16[2,128,4,8,2,6]{1,4,5,3,2,0:T(2,128)(2,1)} %param.4) | data formatting | bytes 393216 | tf_op args[1]
  1.1 15.1 %all_to_all.66 = bf16[2,128,4,8,2,6]{1,4,5,2,0,3:T(2,128)(2,1)S(1)} all-to-all(bf16[2,128,4,8,2,6]{1,4,5,2,0,3:T(2,128)(2,1)S(1)} %copy.21), channel_id=1, replica_groups=mesh['lat'=8,'rep'=4] {'lat'}, dimensions={3} | all-to-all | bytes 393216 | tf_op jit(solution)/shard_map/all_to_all | solution.py:43
  16.1 0.1 copy.29
  16.2 0.7 reshape.161
  16.9 3.4 %all-to-all-start.2 = ((bf16[2,1024,4,1,2,6]{1,4,5,0,3,2:T(2,128)(2,1)}), bf16[2,1024,4,1,2,6]{1,4,5,0,3,2:T(2,128)(2,1)S(1)}, u32[]{:S(2)}, u32[]{:S(2)}) async-start(bf16[2,1024,4,1,2,6]{1,4,5,0,3,2:T(2,128)(2,1)} %reshape.161), calls=%async_computation.2 | async-start | bytes 393216 | tf_op jit(solution)/shard_map/all_to_all | solution.py:42
  20.3 3.2 %copy.19 = bf16[128,1,8,1025]{0,3,1,2:T(8,128)(2,1)} copy(bf16[128,1,8,1025]{0,2,3,1:T(8,128)(2,1)} %param.3) | data formatting | bytes 4198400 | tf_op args[0]
  23.5 2.1 %all-to-all-done.2 = bf16[2,1024,4,1,2,6]{1,4,5,0,3,2:T(2,128)(2,1)S(1)} async-done(((bf16[2,1024,4,1,2,6]{1,4,5,0,3,2:T(2,128)(2,1)}), bf16[2,1024,4,1,2,6]{1,4,5,0,3,2:T(2,128)(2,1)S(1)}, u32[]{:S(2)}, u32[]{:S(2)}) %all-to-all-start.2) | async-done | bytes 196640 | tf_op jit(solution)/shard_map/all_to_all | solution.py:42
  25.6 3.6 %all-to-all-start = ((bf16[128,1,8,1025]{0,3,1,2:T(8,128)(2,1)}), bf16[128,1,8,1025]{0,3,1,2:T(8,128)(2,1)S(1)}, u32[]{:S(2)}, u32[]{:S(2)}) async-start(bf16[128,1,8,1025]{0,3,1,2:T(8,128)(2,1)} %copy.19), calls=%async_computation | async-start | bytes 4227072 | tf_op jit(solution)/shard_map/all_to_all | solution.py:41
  29.2 1.3 %dynamic_slice.4 = s32[1,1]{1,0:T(1,128)} dynamic-slice(s32[4,8]{1,0:T(4,128)} %param.5, s32[]{:T(128)S(6)} %select_n.34, s32[]{:T(128)S(6)} %select_n.36), dynamic_slice_sizes={1,1} | dynamic-slice | bytes 12 | tf_op jit(solution)/shard_map/dynamic_slice | solution.py:40
  31.2 0.1 fusion.22
  31.3 0.1 fusion.24
  31.4 0.1 fusion.23
  31.6 0.1 fusion.14
  31.7 45.8 %all-to-all-done = bf16[128,1,8,1025]{0,3,1,2:T(8,128)(2,1)S(1)} async-done(((bf16[128,1,8,1025]{0,3,1,2:T(8,128)(2,1)}), bf16[128,1,8,1025]{0,3,1,2:T(8,128)(2,1)S(1)}, u32[]{:S(2)}, u32[]{:S(2)}) %all-to-all-start) | async-done | bytes 2099232 | tf_op jit(solution)/shard_map/all_to_all | solution.py:41
  77.4 3.8 %copy.61 = bf16[8,128,1,1,1025]{1,0,4,3,2:T(8,128)(2,1)S(1)} copy(bf16[8,128,1,1,1025]{1,4,0,3,2:T(8,128)(2,1)S(1)} %bitcast.44) | data formatting | bytes 4198400 | tf_op jit(solution)/shard_map/all_to_all | solution.py:41
  81.2 0.2 pad.4
  81.5 0.6 copy.35
  82.1 2.5 %fusion.4 = f32[1,1,1025,24]{2,3,1,0:T(8,128)S(1)} fusion(bf16[4,1025]{1,0:T(4,128)(2,1)S(1)} %fusion.18, bf16[1024,1025]{0,1:T(8,128)(2,1)S(1)} %bitcast.46, bf16[1024,1,24]{0,2,1:T(8,128)(2,1)S(1)} %get-tuple-element.15, bf16[1024,1,24]{0,2,1:T(8,128)(2,1)S(1)} %get-tuple-element.16, bf16[1024,1,24]{0,2,1:T(8,128)(2,1)S(1)} %get-tuple-element.6, ...), kind=kOutput, calls=%fused_computation.4 | convolution fusion | flops 206016512 | bytes 2402408 | tf_op jit(solution)/shard_map/ljoqc,ljoqf->jocf/dot_general | solution.py:34
  84.6 0.1 copy.28
  84.7 6.8 %all_to_all.67 = f32[1,1,1025,24]{2,1,0,3:T(1,128)S(1)} all-to-all(f32[1,1,1025,24]{2,1,0,3:T(1,128)S(1)} %copy.28), channel_id=1, replica_groups=mesh['lat'=8,'rep'=4] {'rep'}, dimensions={3} | all-to-all | bytes 196800 | tf_op jit(solution)/shard_map/all_to_all | solution.py:50
  91.5 0.6 copy.63
  (2 shorter events, 0.0 us)
Async XLA Ops:
  16.9 8.6 %all-to-all-start.2 = ((bf16[2,1024,4,1,2,6]{1,4,5,0,3,2:T(2,128)(2,1)}), bf16[2,1024,4,1,2,6]{1,4,5,0,3,2:T(2,128)(2,1)S(1)}, u32[]{:S(2)}, u32[]{:S(2)}) async-start(bf16[2,1024,4,1,2,6]{1,4,5,0,3,2:T(2,128)(2,1)} %reshape.161), calls=%async_computation.2 | async-start | bytes 393216 | tf_op jit(solution)/shard_map/all_to_all | solution.py:42
  25.6 51.9 %all-to-all-start = ((bf16[128,1,8,1025]{0,3,1,2:T(8,128)(2,1)}), bf16[128,1,8,1025]{0,3,1,2:T(8,128)(2,1)S(1)}, u32[]{:S(2)}, u32[]{:S(2)}) async-start(bf16[128,1,8,1025]{0,3,1,2:T(8,128)(2,1)} %copy.19), calls=%async_computation | async-start | bytes 4227072 | tf_op jit(solution)/shard_map/all_to_all | solution.py:41
where the time goes:
time: 92.5 us; the launch traced here: 92.1 us
  waiting for transfers between devices  47.8 us (52%)
  blocking collectives  21.8 us (24%)
  local copies, waits for them, and re-layouts  12.2 us (13%)
  starting transfers between devices  6.97 us (8%)
  matrix products  2.46 us (3%)
    all_to_all x1, waiting for transfers between devices, per_device(): lax.all_to_all(legendre_table, 'lat', split_axis=2, concat_axis=0, tiled=...  45.8 us
    all_to_all x1, blocking collectives, per_device(): lax.all_to_all(fourier, 'lat', split_axis=3, concat_axis=1, tiled=True)  15.1 us
    all_to_all x1, blocking collectives, per_device(): lax.all_to_all(owned, 'rep', split_axis=3, concat_axis=0, tiled=True)  6.76 us
    unnamed x5, local copies, waits for them, and re-layouts  5.77 us
    all_to_all x1, local copies, waits for them, and re-layouts, per_device(): lax.all_to_all(legendre_table, 'lat', split_axis=2, concat_axis=0, tiled=...  3.8 us
    all_to_all x1, starting transfers between devices, per_device(): lax.all_to_all(legendre_table, 'lat', split_axis=2, concat_axis=0, tiled=...  3.6 us
    all_to_all x1, starting transfers between devices, per_device(): lax.all_to_all(lax.all_to_all(fourier, 'lat', split_axis=3, concat_axis=1...  3.36 us
    dot_general x1, matrix products, local_sums(): jnp.einsum('ljoqc,ljoqf->jocf', masked, combos, preferred_element_type=jn...  2.46 us
  transfers between devices with their start and end apart: 2, of which 2 were waited for; matrix products, arithmetic and copies ran while one was open for 5% of the time, Pallas kernels for 0%

commit v1 on v0

--- a/solution.py
+++ b/solution.py
@@ -1,14 +1,20 @@
+import functools
+
 import jax
 import jax.numpy as jnp
 from jax import lax
+from jax.experimental import pallas as pl
+from jax.experimental.pallas import tpu as pltpu
 from jax.sharding import PartitionSpec as P
 
-TRUNC = 1024
+MESH = pl.DeviceIdType.MESH
+LANES = 128
+SUB = 8
 
 
 def selector(lows, width):
     column = jnp.arange(width, dtype=jnp.int32)
-    split = (TRUNC - lows)[..., None]
+    split = (width - 1 - lows)[..., None]
     upper = column >= split
     offset = jnp.where(upper, column - split, column)
     index = 2 * upper.astype(jnp.int32) + offset % 2
@@ -34,7 +40,7 @@
     return jnp.einsum("ljoqc,ljoqf->jocf", masked, combos, preferred_element_type=jnp.float32)
 
 
-def per_device(legendre_table, fourier, pair_low):
+def moved_table(legendre_table, fourier, pair_low):
     quarter = legendre_table.shape[1]
     lows_blk = lax.dynamic_slice_in_dim(pair_low, lax.axis_index("rep") * quarter, quarter, 0)
     lows_own = lax.dynamic_slice_in_dim(lows_blk, lax.axis_index("lat"), 1, 1)
@@ -47,11 +53,213 @@
         tiled=True,
     )
     owned = local_sums(table_blk, fourier_blk, lows_own)
-    spectral = lax.all_to_all(owned, "rep", split_axis=3, concat_axis=0, tiled=True)
-    return spectral
+    return lax.all_to_all(owned, "rep", split_axis=3, concat_axis=0, tiled=True)
+
+
+def kernel(
+    nlat, nrep, cols, trunc,
+    low_ref, table_ref, mine_ref, out_ref,
+    raw, wide, split, combos, block, outgoing, incoming, total,
+    load_sem, give_sem, take_sem, send_sem, recv_sem,
+):
+    me_l, me_r = lax.axis_index("lat"), lax.axis_index("rep")
+    tiles = trunc // LANES
+    rows = LANES * nlat
+    n = nlat * nrep
+    me = me_l * nrep + me_r
+
+    barrier = pltpu.get_barrier_semaphore()
+
+    @pl.loop(1, n)
+    def _(k):
+        peer = lax.rem(me + k, n)
+        pl.semaphore_signal(barrier, inc=1, device_id=(peer // nrep, lax.rem(peer, nrep)), device_id_type=MESH)
+
+    def load(i, count):
+        part = pl.ds(pl.multiple_of(i * rows, rows), count)
+        return pltpu.make_async_copy(table_ref.at[part], raw.at[part], load_sem.at[i])
+
+    @pl.loop(0, tiles)
+    def _(i):
+        load(i, rows).start()
+
+    load(tiles, nlat).start()
+    block[...] = jnp.zeros_like(block)
+    combos[me_r] = mine_ref[me_r]
+
+    pl.semaphore_wait(barrier, n - 1)
+
+    def give(k):
+        other = lax.rem(me_r + k, nrep)
+        return pltpu.make_async_remote_copy(
+            src_ref=mine_ref.at[other],
+            dst_ref=combos.at[me_r],
+            send_sem=give_sem.at[other],
+            recv_sem=take_sem.at[me_r],
+            device_id=(me_l, other),
+            device_id_type=MESH,
+        )
+
+    def take(k):
+        other = lax.rem(me_r + k, nrep)
+        return pltpu.make_async_remote_copy(
+            src_ref=mine_ref.at[other],
+            dst_ref=combos.at[other],
+            send_sem=give_sem.at[other],
+            recv_sem=take_sem.at[other],
+            device_id=(me_l, other),
+            device_id_type=MESH,
+        )
+
+    for k in range(1, nrep):
+        give(k).start()
+
+    @pl.loop(0, tiles)
+    def _(i):
+        load(i, rows).wait()
+        wide[...] = raw[pl.ds(pl.multiple_of(i * rows, rows), rows), :].astype(jnp.float32)
+        for o in range(nlat):
+            split[o, pl.ds(pl.multiple_of(i * LANES, LANES), LANES), :] = wide[pl.ds(o, LANES, stride=nlat), :].astype(jnp.bfloat16)
+
+    load(tiles, nlat).wait()
+    last = raw[rows * tiles:, :].astype(jnp.float32)
+    for o in range(nlat):
+        split[o, tiles * LANES:, :] = jnp.broadcast_to(last[o:o + 1], (LANES, LANES)).astype(jnp.bfloat16)
+
+    for k in range(1, nrep):
+        take(k).wait_recv()
+
+    def send(o, r):
+        return pltpu.make_async_remote_copy(
+            src_ref=outgoing.at[o, r],
+            dst_ref=incoming.at[me_l, me_r],
+            send_sem=send_sem.at[o, r],
+            recv_sem=recv_sem.at[me_l, me_r],
+            device_id=(o, r),
+            device_id_type=MESH,
+        )
+
+    lane = lax.broadcasted_iota(jnp.int32, (SUB, LANES), 1)
+
+    @pl.loop(0, nlat)
+    def _(k):
+        o = lax.rem(me_l + nlat // 2 + k, nlat)
+        edge = trunc - low_ref[me_r, o]
+        left = jnp.concatenate([combos[r, o] for r in range(nrep)], axis=0)
+        for t in range(tiles + 1):
+            got = lax.dot_general(
+                left, split[o, t * LANES:(t + 1) * LANES, :], (((1,), (1,)), ((), ())),
+                preferred_element_type=jnp.float32,
+            )
+            column = lane + t * LANES if t < tiles else jnp.full_like(lane, trunc)
+            upper = column >= edge
+            odd = (jnp.where(upper, column - edge, column) & 1) == 1
+            for r in range(nrep):
+                q = [got[(4 * r + s) * SUB:(4 * r + s + 1) * SUB] for s in range(4)]
+                value = jnp.where(upper, jnp.where(odd, q[3], q[2]), jnp.where(odd, q[1], q[0]))
+                block[r, t * cols:(t + 1) * cols, :] = value[:cols]
+        for r in range(nrep):
+            outgoing[o, r] = block[r].astype(jnp.bfloat16)
+        for r in range(nrep):
+            @pl.when(jnp.logical_or(o != me_l, r != me_r))
+            def _():
+                send(o, r).start()
+
+    incoming[me_l, me_r] = outgoing[me_l, me_r]
+
+    def receive(l, r):
+        return pltpu.make_async_remote_copy(
+            src_ref=outgoing.at[l, r],
+            dst_ref=incoming.at[l, r],
+            send_sem=send_sem.at[l, r],
+            recv_sem=recv_sem.at[l, r],
+            device_id=(l, r),
+            device_id_type=MESH,
+        )
+
+    @pl.loop(0, nrep)
+    def _(j):
+        for l in range(nlat):
+            @pl.when(jnp.logical_or(l != me_l, j != me_r))
+            def _():
+                receive(l, j).wait_recv()
+        acc = incoming[0, j].astype(jnp.float32)
+        for l in range(1, nlat):
+            acc = acc + incoming[l, j].astype(jnp.float32)
+        total[...] = acc
+        for t in range(tiles):
+            out_ref[j, :, t * LANES:(t + 1) * LANES] = total[t * cols:(t + 1) * cols, :]
+        out_ref[j, :, tiles * LANES:] = total[tiles * cols:(tiles + 1) * cols, 0:1]
+
+    for k in range(1, nrep):
+        give(k).wait_send()
+
+    @pl.loop(1, n)
+    def _(k):
+        peer = lax.rem(me + k, n)
+        send(peer // nrep, lax.rem(peer, nrep)).wait_send()
+
+
+def kept_table(nlat, nrep, legendre_table, fourier, pair_low):
+    lats, _, owners, width = legendre_table.shape
+    slots, cols = fourier.shape[2], fourier.shape[5]
+    trunc = width - 1
+    table = jnp.transpose(legendre_table[:, 0], (2, 1, 0)).reshape(width * owners, lats)
+    mine = jnp.transpose(combine(fourier), (1, 2, 3, 4, 0))
+    mine = jnp.pad(mine, ((0, 0), (0, 0), (0, 0), (0, SUB - cols), (0, 0)))
+    mine = mine.reshape(slots, owners, 4 * SUB, lats)
+    tiles = trunc // LANES
+    height = -(-(tiles + 1) * cols // SUB) * SUB
+    bf16, f32 = jnp.bfloat16, jnp.float32
+    vmem = pl.BlockSpec(memory_space=pltpu.VMEM)
+    out = pl.pallas_call(
+        functools.partial(kernel, nlat, nrep, cols, trunc),
+        out_shape=jax.ShapeDtypeStruct((slots, cols, width), f32),
+        in_specs=[pl.BlockSpec(memory_space=pltpu.SMEM), pl.BlockSpec(memory_space=pl.ANY), vmem],
+        out_specs=vmem,
+        scratch_shapes=[
+            pltpu.VMEM((width * owners, lats), bf16),
+            pltpu.VMEM((LANES * owners, lats), f32),
+            pltpu.VMEM((owners, trunc + LANES, lats), bf16),
+            pltpu.VMEM((nrep, owners, 4 * SUB, lats), bf16),
+            pltpu.VMEM((nrep, height, LANES), f32),
+            pltpu.VMEM((nlat, nrep, height, LANES), bf16),
+            pltpu.VMEM((nlat, nrep, height, LANES), bf16),
+            pltpu.VMEM((height, LANES), f32),
+            pltpu.SemaphoreType.DMA((tiles + 1,)),
+            pltpu.SemaphoreType.DMA((nrep,)),
+            pltpu.SemaphoreType.DMA((nrep,)),
+            pltpu.SemaphoreType.DMA((nlat, nrep)),
+            pltpu.SemaphoreType.DMA((nlat, nrep)),
+        ],
+        compiler_params=pltpu.CompilerParams(collective_id=0, has_side_effects=True),
+        cost_estimate=pl.CostEstimate(
+            flops=2 * 4 * nrep * SUB * lats * owners * (trunc + LANES),
+            bytes_accessed=2 * width * owners * lats,
+            transcendentals=0,
+        ),
+    )(pair_low, table, mine)
+    return jnp.transpose(out, (0, 2, 1))[:, None]
 
 
 def solution(mesh):
+    nlat, nrep = mesh.shape["lat"], mesh.shape["rep"]
+
+    def per_device(legendre_table, fourier, pair_low):
+        lats, quarter, owners, width = legendre_table.shape
+        fits = (
+            lats == LANES
+            and quarter == 1
+            and owners == nlat
+            and nlat == SUB
+            and fourier.shape[2] == nrep
+            and fourier.shape[5] <= SUB
+            and (width - 1) % LANES == 0
+        )
+        if fits:
+            return kept_table(nlat, nrep, legendre_table, fourier, pair_low)
+        return moved_table(legendre_table, fourier, pair_low)
+
     return jax.shard_map(
         per_device,
         mesh=mesh,

time: 92.5 us -> 30.7 us (0.33)
  waiting for transfers between devices: 47.8 us -> 0 us
  Pallas kernels: 0 us -> 26.2 us
  blocking collectives: 21.8 us -> 0 us
  local copies, waits for them, and re-layouts: 12.2 us -> 2.46 us
  starting transfers between devices: 6.97 us -> 0 us
  matrix products: 2.46 us -> 0 us
  other arithmetic: 0.09 us -> 1.85 us
    all_to_all x2 -> x0, waiting for transfers between devices: 47.8 us -> none  [the longest x1 45.8 us: per_device(): lax.all_to_all(legendre_table, 'lat', split_axis=2, concat_axis=0, tiled=...]
    pallas_call x0 -> x1, Pallas kernels: none -> 26.2 us  [kept_table(): pl.pallas_call(functools.partial(kernel, nlat, nrep, cols, trunc), out_sh...]
    all_to_all x2 -> x0, blocking collectives: 21.8 us -> none  [the longest x1 15.1 us: per_device(): lax.all_to_all(fourier, 'lat', split_axis=3, concat_axis=1, tiled=True)]
    all_to_all x2 -> x0, starting transfers between devices: 6.97 us -> none  [the longest x1 3.6 us: per_device(): lax.all_to_all(legendre_table, 'lat', split_axis=2, concat_axis=0, tiled=...]
    unnamed x5 -> x1, local copies, waits for them, and re-layouts: 5.77 us -> 0.05 us
    all_to_all x3 -> x0, local copies, waits for them, and re-layouts: 4.61 us -> none  [the longest x1 3.8 us: per_device(): lax.all_to_all(legendre_table, 'lat', split_axis=2, concat_axis=0, tiled=...]
    dot_general x1 -> x0, matrix products: 2.46 us -> none  [local_sums(): jnp.einsum('ljoqc,ljoqf->jocf', masked, combos, preferred_element_type=jn...]
    broadcast_in_dim x0 -> x1, local copies, waits for them, and re-layouts: none -> 1.67 us  [kept_table(): return jnp.transpose(out, (0, 2, 1))[:, None]]
  transfers between devices with their start and end apart: 2 -> 0, of which waited for: 2 -> 0; matrix products, arithmetic and copies ran while one was open for 5% -> 0% of each run, Pallas kernels for 0% -> 0%
where the time goes in v1:
time: 30.7 us; the launch traced here: 30.6 us
  Pallas kernels  26.2 us (85%)
  local copies, waits for them, and re-layouts  2.46 us (8%)
  other arithmetic  1.85 us (6%)
    pallas_call x1, Pallas kernels, kept_table(): pl.pallas_call(functools.partial(kernel, nlat, nrep, cols, trunc), out_sh...  26.2 us
    broadcast_in_dim x1, local copies, waits for them, and re-layouts, kept_table(): return jnp.transpose(out, (0, 2, 1))[:, None]  1.67 us
    convert_element_type x1, other arithmetic, combine(): north = fourier[0].astype(jnp.float32)  1.08 us
    reshape x1, local copies, waits for them, and re-layouts, kept_table(): mine = mine.reshape(slots, owners, 4 * SUB, lats)  0.74 us

profile of v1, /device:TPU:0, one launch (start us, length us, event | category | flops | bytes accessed | tf_op | source)
XLA Modules:
  0.0 30.6 jit_solution(15991364319601250160)
XLA Ops:
  0.0 1.1 %bitcast_convert_fusion.1 = (f32[128,4,8,2,6]{0,3,4,2,1:T(2,128)S(1)}, f32[128,4,8,2,6]{0,3,4,2,1:T(2,128)S(1)}) fusion(bf16[2,128,4,8,2,6]{1,4,5,3,2,0:T(2,128)(2,1)} %param.4), kind=kLoop, calls=%fused_computation.3 | loop fusion | flops 98304 | bytes 589824 | tf_op jit(solution)/shard_map/convert_element_type | solution.py:25
  1.1 0.3 %add_convert_fusion.1 = (bf16[128,4,8,1,6]{0,3,4,2,1:T(2,128)(2,1)S(1)}, bf16[128,4,8,1,6]{0,3,4,2,1:T(2,128)(2,1)S(1)}, bf16[128,4,8,1,6]{0,3,4,2,1:T(2,128)(2,1)S(1)}, bf16[128,4,8,1,6]{0,3,4,2,1:T(2,128)(2,1)S(1)}) fusion(f32[128,4,8,2,6]{0,3,4,2,1:T(2,128)S(1)} %get-tuple-element.10, f32[128,4,8,2,6]{0,3,4,2,1:T(2,128)S(1)} %get-tuple-element.9), kind=kLoop, calls=%fused_computation.7 | loop fusion | flops 196608 | bytes 589824 | tf_op jit(solution)/shard_map/convert.2
  1.4 0.5 %maximum_bitcast_fusion = bf16[4,8,4,6,128]{4,2,3,1,0:T(4,128)(2,1)S(1)} fusion(bf16[128,4,8,1,6]{0,3,4,2,1:T(2,128)(2,1)S(1)} %get-tuple-element.7, bf16[128,4,8,1,6]{0,3,4,2,1:T(2,128)(2,1)S(1)} %get-tuple-element.8, bf16[128,4,8,1,6]{0,3,4,2,1:T(2,128)(2,1)S(1)} %get-tuple-element.6, bf16[128,4,8,1,6]{0,3,4,2,1:T(2,128)(2,1)S(1)} %get-tuple-element.5), kind=kLoop, calls=%fused_computation.1 | loop fusion | flops 786432 | bytes 393216 | tf_op jit(solution)/shard_map/transpose | solution.py:208
  1.9 0.1 copy.6
  1.9 0.7 %pad_bitcast_fusion.mine_ref = bf16[4,8,32,128]{3,2,1,0:T(8,128)(2,1)} fusion(bf16[4,8,4,6,128]{4,3,2,1,0:T(8,128)(2,1)S(1)} %copy.6), kind=kLoop, calls=%fused_computation | loop fusion | bytes 458752 | tf_op jit(solution)/shard_map/reshape | solution.py:210
  2.7 26.2 %shard_map.37 = f32[4,6,1025]{2,1,0:T(8,128)} custom-call(s32[4,8]{1,0:T(4,128)} %low_ref.1, bf16[8200,128]{1,0:T(8,128)(2,1)} %bitcast.18, bf16[4,8,32,128]{3,2,1,0:T(8,128)(2,1)} %pad_bitcast_fusion.mine_ref), custom_call_target="tpu_custom_call" | custom-call | flops 301989888 | bytes 2099200 | tf_op jit(solution)/shard_map/pallas_call | solution.py:215
  28.9 1.7 %copy.5 = f32[4,1,1025,6]{2,1,3,0:T(1,128)} copy(f32[4,1,1025,6]{2,3,0,1:T(8,128)} %bitcast.19) | data formatting | bytes 196800 | tf_op jit(solution)/shard_map/broadcast_in_dim | solution.py:242

commit v2 on v1

--- a/solution.py
+++ b/solution.py
@@ -58,9 +58,9 @@
 
 def kernel(
     nlat, nrep, cols, trunc,
-    low_ref, table_ref, mine_ref, out_ref,
-    raw, wide, split, combos, block, outgoing, incoming, total,
-    load_sem, give_sem, take_sem, send_sem, recv_sem,
+    low_hbm, table_ref, four_hbm, out_ref,
+    low_ref, four_ref, raw, wide, split, mine, combos, block, outgoing, incoming, total,
+    low_sem, four_sem, load_sem, give_sem, take_sem, send_sem, recv_sem,
 ):
     me_l, me_r = lax.axis_index("lat"), lax.axis_index("rep")
     tiles = trunc // LANES
@@ -69,6 +69,10 @@
     me = me_l * nrep + me_r
 
     barrier = pltpu.get_barrier_semaphore()
+    get_four = pltpu.make_async_copy(four_hbm, four_ref, four_sem)
+    get_low = pltpu.make_async_copy(low_hbm, low_ref, low_sem)
+    get_four.start()
+    get_low.start()
 
     @pl.loop(1, n)
     def _(k):
@@ -85,14 +89,28 @@
 
     load(tiles, nlat).start()
     block[...] = jnp.zeros_like(block)
-    combos[me_r] = mine_ref[me_r]
+
+    pairs = four_ref.shape[2]
+    to = lax.broadcasted_iota(jnp.int32, (nlat * 4 * SUB, pairs), 0)
+    frm = lax.broadcasted_iota(jnp.int32, (nlat * 4 * SUB, pairs), 1)
+    o_to, q_to, f_to = to // (4 * SUB), lax.rem(to // SUB, 4), lax.rem(to, SUB)
+    hit = (f_to < cols) & (frm == (o_to * cols + f_to) * 2 + q_to // 2)
+    north = jnp.where(hit, 1.0, 0.0).astype(jnp.bfloat16)
+    south = jnp.where(hit, jnp.where(lax.rem(q_to, 2) == 1, -1.0, 1.0), 0.0).astype(jnp.bfloat16)
+    get_four.wait()
+    get_low.wait()
+    for r in range(nrep):
+        both = jnp.dot(north, four_ref[0, r], preferred_element_type=jnp.float32)
+        both = both + jnp.dot(south, four_ref[1, r], preferred_element_type=jnp.float32)
+        mine[r] = both.astype(jnp.bfloat16).reshape(nlat, 4 * SUB, LANES)
+    combos[me_r] = mine[me_r]
 
     pl.semaphore_wait(barrier, n - 1)
 
     def give(k):
         other = lax.rem(me_r + k, nrep)
         return pltpu.make_async_remote_copy(
-            src_ref=mine_ref.at[other],
+            src_ref=mine.at[other],
             dst_ref=combos.at[me_r],
             send_sem=give_sem.at[other],
             recv_sem=take_sem.at[me_r],
@@ -103,7 +121,7 @@
     def take(k):
         other = lax.rem(me_r + k, nrep)
         return pltpu.make_async_remote_copy(
-            src_ref=mine_ref.at[other],
+            src_ref=mine.at[other],
             dst_ref=combos.at[other],
             send_sem=give_sem.at[other],
             recv_sem=take_sem.at[other],
@@ -140,6 +158,7 @@
         )
 
     lane = lax.broadcasted_iota(jnp.int32, (SUB, LANES), 1)
+    row = lax.broadcasted_iota(jnp.int32, (SUB, LANES), 0)
 
     @pl.loop(0, nlat)
     def _(k):
@@ -157,7 +176,10 @@
             for r in range(nrep):
                 q = [got[(4 * r + s) * SUB:(4 * r + s + 1) * SUB] for s in range(4)]
                 value = jnp.where(upper, jnp.where(odd, q[3], q[2]), jnp.where(odd, q[1], q[0]))
-                block[r, t * cols:(t + 1) * cols, :] = value[:cols]
+                if t < tiles:
+                    block[r, t * cols:(t + 1) * cols, :] = value[:cols]
+                else:
+                    block[r, t * cols:t * cols + 1, :] = jnp.sum(jnp.where(lane == row, value, 0.0), axis=0, keepdims=True)
         for r in range(nrep):
             outgoing[o, r] = block[r].astype(jnp.bfloat16)
         for r in range(nrep):
@@ -188,8 +210,10 @@
             acc = acc + incoming[l, j].astype(jnp.float32)
         total[...] = acc
         for t in range(tiles):
-            out_ref[j, :, t * LANES:(t + 1) * LANES] = total[t * cols:(t + 1) * cols, :]
-        out_ref[j, :, tiles * LANES:] = total[tiles * cols:(tiles + 1) * cols, 0:1]
+            out_ref[j, :, 0, t * LANES:(t + 1) * LANES] = total[t * cols:(t + 1) * cols, :]
+        ends = jnp.broadcast_to(total[tiles * cols:tiles * cols + 1, :], (SUB, LANES))
+        ends = jnp.sum(jnp.where(lane == row, ends, 0.0), axis=1, keepdims=True)
+        out_ref[j, :, 0, tiles * LANES:] = ends[:cols]
 
     for k in range(1, nrep):
         give(k).wait_send()
@@ -205,41 +229,44 @@
     slots, cols = fourier.shape[2], fourier.shape[5]
     trunc = width - 1
     table = jnp.transpose(legendre_table[:, 0], (2, 1, 0)).reshape(width * owners, lats)
-    mine = jnp.transpose(combine(fourier), (1, 2, 3, 4, 0))
-    mine = jnp.pad(mine, ((0, 0), (0, 0), (0, 0), (0, SUB - cols), (0, 0)))
-    mine = mine.reshape(slots, owners, 4 * SUB, lats)
+    columns = jnp.transpose(fourier, (0, 2, 3, 5, 4, 1)).reshape(2, slots, owners * cols * 2, lats)
     tiles = trunc // LANES
-    height = -(-(tiles + 1) * cols // SUB) * SUB
+    height = tiles * cols + 2
     bf16, f32 = jnp.bfloat16, jnp.float32
     vmem = pl.BlockSpec(memory_space=pltpu.VMEM)
     out = pl.pallas_call(
         functools.partial(kernel, nlat, nrep, cols, trunc),
-        out_shape=jax.ShapeDtypeStruct((slots, cols, width), f32),
-        in_specs=[pl.BlockSpec(memory_space=pltpu.SMEM), pl.BlockSpec(memory_space=pl.ANY), vmem],
+        out_shape=jax.ShapeDtypeStruct((slots, cols, 1, width), f32),
+        in_specs=[pl.BlockSpec(memory_space=pltpu.HBM)] * 3,
         out_specs=vmem,
         scratch_shapes=[
+            pltpu.SMEM(pair_low.shape, jnp.int32),
+            pltpu.VMEM(columns.shape, bf16),
             pltpu.VMEM((width * owners, lats), bf16),
             pltpu.VMEM((LANES * owners, lats), f32),
             pltpu.VMEM((owners, trunc + LANES, lats), bf16),
+            pltpu.VMEM((nrep, owners, 4 * SUB, lats), bf16),
             pltpu.VMEM((nrep, owners, 4 * SUB, lats), bf16),
             pltpu.VMEM((nrep, height, LANES), f32),
             pltpu.VMEM((nlat, nrep, height, LANES), bf16),
             pltpu.VMEM((nlat, nrep, height, LANES), bf16),
             pltpu.VMEM((height, LANES), f32),
+            pltpu.SemaphoreType.DMA,
+            pltpu.SemaphoreType.DMA,
             pltpu.SemaphoreType.DMA((tiles + 1,)),
             pltpu.SemaphoreType.DMA((nrep,)),
             pltpu.SemaphoreType.DMA((nrep,)),
             pltpu.SemaphoreType.DMA((nlat, nrep)),
             pltpu.SemaphoreType.DMA((nlat, nrep)),
         ],
-        compiler_params=pltpu.CompilerParams(collective_id=0, has_side_effects=True),
+        compiler_params=pltpu.CompilerParams(collective_id=0, has_side_effects=True, vmem_limit_bytes=55000 << 10),
         cost_estimate=pl.CostEstimate(
             flops=2 * 4 * nrep * SUB * lats * owners * (trunc + LANES),
             bytes_accessed=2 * width * owners * lats,
             transcendentals=0,
         ),
-    )(pair_low, table, mine)
-    return jnp.transpose(out, (0, 2, 1))[:, None]
+    )(pair_low, table, columns)
+    return jnp.transpose(out, (0, 2, 3, 1))
 
 
 def solution(mesh):

time: 30.7 us -> 25.9 us (0.84)
  other arithmetic: 1.85 us -> 0 us
  Pallas kernels: 26.2 us -> 24.4 us
  local copies, waits for them, and re-layouts: 2.46 us -> 1.33 us
    pallas_call x1, Pallas kernels: 26.2 us -> 24.4 us  [kept_table(): pl.pallas_call(functools.partial(kernel, nlat, nrep, cols, trunc), out_sh...]
    broadcast_in_dim x1 -> x0, local copies, waits for them, and re-layouts: 1.67 us -> none  [kept_table(): return jnp.transpose(out, (0, 2, 1))[:, None]]
    unnamed x1 -> x3, local copies, waits for them, and re-layouts: 0.05 us -> 1.33 us
    convert_element_type x1 -> x0, other arithmetic: 1.08 us -> none  [combine(): north = fourier[0].astype(jnp.float32)]
    reshape x1 -> x0, local copies, waits for them, and re-layouts: 0.74 us -> none  [kept_table(): mine = mine.reshape(slots, owners, 4 * SUB, lats)]
    transpose x1 -> x0, other arithmetic: 0.46 us -> none  [kept_table(): mine = jnp.transpose(combine(fourier), (1, 2, 3, 4, 0))]
    another operation x1 -> x0, other arithmetic: 0.31 us -> none
where the time goes in v2:
time: 25.9 us; the launch traced here: 25.8 us
  Pallas kernels  24.4 us (94%)
  local copies, waits for them, and re-layouts  1.33 us (5%)
    pallas_call x1, Pallas kernels, kept_table(): pl.pallas_call(functools.partial(kernel, nlat, nrep, cols, trunc), out_sh...  24.4 us
    unnamed x3, local copies, waits for them, and re-layouts  1.33 us

profile of v2, /device:TPU:0, one launch (start us, length us, event | category | flops | bytes accessed | tf_op | source)
XLA Modules:
  0.0 25.8 jit_solution(4305183566144615805)
XLA Ops:
  0.0 0.0 copy-start
  0.0 0.7 %copy-done = s32[4,8]{1,0:T(4,128)S(1)} copy-done((s32[4,8]{1,0:T(4,128)S(1)}, s32[4,8]{1,0:T(4,128)}, u32[]{:S(2)}) %copy-start) | copy-done | bytes 152
  0.7 24.4 %shard_map.37 = f32[4,6,1,1025]{3,2,1,0:T(1,128)S(1)} custom-call(s32[4,8]{1,0:T(4,128)S(1)} %copy-done, bf16[8200,128]{1,0:T(8,128)(2,1)} %bitcast.10, bf16[2,4,96,128]{3,2,1,0:T(8,128)(2,1)} %bitcast.11), custom_call_target="tpu_custom_call" | custom-call | flops 301989888 | bytes 2099200 | tf_op jit(solution)/shard_map/pallas_call | solution.py:237
  25.1 0.6 %copy.5 = f32[4,1,1025,6]{2,1,3,0:T(1,128)} copy(f32[4,1,1025,6]{2,1,3,0:T(1,128)S(1)} %bitcast.9) | data formatting | bytes 196800
Async XLA Ops:
  0.0 0.7 %copy-start = (s32[4,8]{1,0:T(4,128)S(1)}, s32[4,8]{1,0:T(4,128)}, u32[]{:S(2)}) copy-start(s32[4,8]{1,0:T(4,128)} %low_hbm.1) | copy-start | bytes 388

commit v3 on v2

--- a/solution.py
+++ b/solution.py
@@ -144,9 +144,6 @@
     for o in range(nlat):
         split[o, tiles * LANES:, :] = jnp.broadcast_to(last[o:o + 1], (LANES, LANES)).astype(jnp.bfloat16)
 
-    for k in range(1, nrep):
-        take(k).wait_recv()
-
     def send(o, r):
         return pltpu.make_async_remote_copy(
             src_ref=outgoing.at[o, r],
@@ -159,12 +156,14 @@
 
     lane = lax.broadcasted_iota(jnp.int32, (SUB, LANES), 1)
     row = lax.broadcasted_iota(jnp.int32, (SUB, LANES), 0)
-
-    @pl.loop(0, nlat)
-    def _(k):
-        o = lax.rem(me_l + nlat // 2 + k, nlat)
+    half = nlat // 2
+
+    def far_first(k):
+        return lax.rem(1 - me_l // half + k // half, 2) * half + lax.rem(me_l + k, half)
+
+    def partial_sums(o, groups):
         edge = trunc - low_ref[me_r, o]
-        left = jnp.concatenate([combos[r, o] for r in range(nrep)], axis=0)
+        left = jnp.concatenate([combos[r, o] for r in groups], axis=0)
         for t in range(tiles + 1):
             got = lax.dot_general(
                 left, split[o, t * LANES:(t + 1) * LANES, :], (((1,), (1,)), ((), ())),
@@ -173,19 +172,35 @@
             column = lane + t * LANES if t < tiles else jnp.full_like(lane, trunc)
             upper = column >= edge
             odd = (jnp.where(upper, column - edge, column) & 1) == 1
-            for r in range(nrep):
-                q = [got[(4 * r + s) * SUB:(4 * r + s + 1) * SUB] for s in range(4)]
+            for i in range(len(groups)):
+                q = [got[(4 * i + s) * SUB:(4 * i + s + 1) * SUB] for s in range(4)]
                 value = jnp.where(upper, jnp.where(odd, q[3], q[2]), jnp.where(odd, q[1], q[0]))
                 if t < tiles:
-                    block[r, t * cols:(t + 1) * cols, :] = value[:cols]
+                    block[i, t * cols:(t + 1) * cols, :] = value[:cols]
                 else:
-                    block[r, t * cols:t * cols + 1, :] = jnp.sum(jnp.where(lane == row, value, 0.0), axis=0, keepdims=True)
-        for r in range(nrep):
-            outgoing[o, r] = block[r].astype(jnp.bfloat16)
-        for r in range(nrep):
-            @pl.when(jnp.logical_or(o != me_l, r != me_r))
-            def _():
-                send(o, r).start()
+                    block[i, t * cols:t * cols + 1, :] = jnp.sum(jnp.where(lane == row, value, 0.0), axis=0, keepdims=True)
+        for i, r in enumerate(groups):
+            outgoing[o, r] = block[i].astype(jnp.bfloat16)
+
+    @pl.loop(0, nlat)
+    def _(k):
+        o = far_first(k)
+        partial_sums(o, [me_r])
+
+        @pl.when(o != me_l)
+        def _():
+            send(o, me_r).start()
+
+    for k in range(1, nrep):
+        take(k).wait_recv()
+
+    @pl.loop(0, nlat)
+    def _(k):
+        o = far_first(k)
+        others = [lax.rem(me_r + i, nrep) for i in range(1, nrep)]
+        partial_sums(o, others)
+        for r in others:
+            send(o, r).start()
 
     incoming[me_l, me_r] = outgoing[me_l, me_r]
 

time: 25.9 us -> 23.9 us (0.923)
  Pallas kernels: 24.4 us -> 22.4 us
    pallas_call x1, Pallas kernels: 24.4 us -> 22.4 us  [kept_table(): pl.pallas_call(functools.partial(kernel, nlat, nrep, cols, trunc), out_sh...]
where the time goes in v3:
time: 23.9 us; the launch traced here: 23.7 us
  Pallas kernels  22.4 us (94%)
  local copies, waits for them, and re-layouts  1.33 us (6%)
    pallas_call x1, Pallas kernels, kept_table(): pl.pallas_call(functools.partial(kernel, nlat, nrep, cols, trunc), out_sh...  22.4 us
    unnamed x3, local copies, waits for them, and re-layouts  1.33 us

profile of v3, /device:TPU:0, one launch (start us, length us, event | category | flops | bytes accessed | tf_op | source)
XLA Modules:
  0.0 23.7 jit_solution(6091806032371515172)
XLA Ops:
  0.0 0.0 copy-start
  0.0 0.7 %copy-done = s32[4,8]{1,0:T(4,128)S(1)} copy-done((s32[4,8]{1,0:T(4,128)S(1)}, s32[4,8]{1,0:T(4,128)}, u32[]{:S(2)}) %copy-start) | copy-done | bytes 152
  0.7 22.4 %shard_map.37 = f32[4,6,1,1025]{3,2,1,0:T(1,128)S(1)} custom-call(s32[4,8]{1,0:T(4,128)S(1)} %copy-done, bf16[8200,128]{1,0:T(8,128)(2,1)} %bitcast.10, bf16[2,4,96,128]{3,2,1,0:T(8,128)(2,1)} %bitcast.11), custom_call_target="tpu_custom_call" | custom-call | flops 301989888 | bytes 2099200 | tf_op jit(solution)/shard_map/pallas_call | solution.py:252
  23.1 0.6 %copy.5 = f32[4,1,1025,6]{2,1,3,0:T(1,128)} copy(f32[4,1,1025,6]{2,1,3,0:T(1,128)S(1)} %bitcast.9) | data formatting | bytes 196800
Async XLA Ops:
  0.0 0.7 %copy-start = (s32[4,8]{1,0:T(4,128)S(1)}, s32[4,8]{1,0:T(4,128)}, u32[]{:S(2)}) copy-start(s32[4,8]{1,0:T(4,128)} %low_hbm.1) | copy-start | bytes 388

commit v4 on v3

--- a/solution.py
+++ b/solution.py
@@ -59,8 +59,8 @@
 def kernel(
     nlat, nrep, cols, trunc,
     low_hbm, table_ref, four_hbm, out_ref,
-    low_ref, four_ref, raw, wide, split, mine, combos, block, outgoing, incoming, total,
-    low_sem, four_sem, load_sem, give_sem, take_sem, send_sem, recv_sem,
+    low_ref, four_ref, raw, wide, split, mine, combos, block, outgoing, incoming, met, total,
+    low_sem, four_sem, load_sem, give_sem, take_sem, send_sem, recv_sem, met_sem,
 ):
     me_l, me_r = lax.axis_index("lat"), lax.axis_index("rep")
     tiles = trunc // LANES
@@ -158,10 +158,26 @@
     row = lax.broadcasted_iota(jnp.int32, (SUB, LANES), 0)
     half = nlat // 2
 
-    def far_first(k):
-        return lax.rem(1 - me_l // half + k // half, 2) * half + lax.rem(me_l + k, half)
-
-    def partial_sums(o, groups):
+    side, parity = me_l // half, lax.rem(me_l, 2)
+    partner = me_l + 1 - 2 * parity
+
+    def near(k):
+        return side * half + lax.rem(me_l + k, half)
+
+    def far(i, which):
+        return (1 - side) * half + 2 * i + which
+
+    def hand(i, r):
+        return pltpu.make_async_remote_copy(
+            src_ref=outgoing.at[far(i, 1 - parity), r],
+            dst_ref=met.at[i, r],
+            send_sem=send_sem.at[far(i, 1 - parity), r],
+            recv_sem=met_sem.at[i, r],
+            device_id=(partner, me_r),
+            device_id_type=MESH,
+        )
+
+    def partial_sums(o, groups, i_met=None):
         edge = trunc - low_ref[me_r, o]
         left = jnp.concatenate([combos[r, o] for r in groups], axis=0)
         for t in range(tiles + 1):
@@ -180,27 +196,40 @@
                 else:
                     block[i, t * cols:t * cols + 1, :] = jnp.sum(jnp.where(lane == row, value, 0.0), axis=0, keepdims=True)
         for i, r in enumerate(groups):
-            outgoing[o, r] = block[i].astype(jnp.bfloat16)
-
-    @pl.loop(0, nlat)
-    def _(k):
-        o = far_first(k)
-        partial_sums(o, [me_r])
-
-        @pl.when(o != me_l)
-        def _():
-            send(o, me_r).start()
-
+            if i_met is None:
+                outgoing[o, r] = block[i].astype(jnp.bfloat16)
+            else:
+                hand(i_met, r).wait_recv()
+                outgoing[o, r] = (block[i] + met[i_met, r].astype(jnp.float32)).astype(jnp.bfloat16)
+
+    def blocks(groups):
+        @pl.loop(0, half // 2)
+        def _(k):
+            i = lax.rem(me_l // 2 + k, half // 2)
+            partial_sums(far(i, 1 - parity), groups)
+            for r in groups:
+                hand(i, r).start()
+
+        @pl.loop(0, half)
+        def _(k):
+            o = near(k)
+            partial_sums(o, groups)
+            for r in groups:
+                @pl.when(jnp.logical_or(o != me_l, r != me_r))
+                def _():
+                    send(o, r).start()
+
+        @pl.loop(0, half // 2)
+        def _(k):
+            i = lax.rem(me_l // 2 + k, half // 2)
+            partial_sums(far(i, parity), groups, i)
+            for r in groups:
+                send(far(i, parity), r).start()
+
+    blocks([me_r])
     for k in range(1, nrep):
         take(k).wait_recv()
-
-    @pl.loop(0, nlat)
-    def _(k):
-        o = far_first(k)
-        others = [lax.rem(me_r + i, nrep) for i in range(1, nrep)]
-        partial_sums(o, others)
-        for r in others:
-            send(o, r).start()
+    blocks([lax.rem(me_r + i, nrep) for i in range(1, nrep)])
 
     incoming[me_l, me_r] = outgoing[me_l, me_r]
 
@@ -216,12 +245,12 @@
 
     @pl.loop(0, nrep)
     def _(j):
-        for l in range(nlat):
+        sources = [side * half + i for i in range(half)] + [far(i, parity) for i in range(half // 2)]
+        acc = jnp.zeros(total.shape, jnp.float32)
+        for l in sources:
             @pl.when(jnp.logical_or(l != me_l, j != me_r))
             def _():
                 receive(l, j).wait_recv()
-        acc = incoming[0, j].astype(jnp.float32)
-        for l in range(1, nlat):
             acc = acc + incoming[l, j].astype(jnp.float32)
         total[...] = acc
         for t in range(tiles):
@@ -265,6 +294,7 @@
             pltpu.VMEM((nrep, height, LANES), f32),
             pltpu.VMEM((nlat, nrep, height, LANES), bf16),
             pltpu.VMEM((nlat, nrep, height, LANES), bf16),
+            pltpu.VMEM((nlat // 4, nrep, height, LANES), bf16),
             pltpu.VMEM((height, LANES), f32),
             pltpu.SemaphoreType.DMA,
             pltpu.SemaphoreType.DMA,
@@ -273,6 +303,7 @@
             pltpu.SemaphoreType.DMA((nrep,)),
             pltpu.SemaphoreType.DMA((nlat, nrep)),
             pltpu.SemaphoreType.DMA((nlat, nrep)),
+            pltpu.SemaphoreType.DMA((nlat // 4, nrep)),
         ],
         compiler_params=pltpu.CompilerParams(collective_id=0, has_side_effects=True, vmem_limit_bytes=55000 << 10),
         cost_estimate=pl.CostEstimate(

time: 23.9 us -> 22.5 us (0.941)
  Pallas kernels: 22.4 us -> 21 us
    pallas_call x1, Pallas kernels: 22.4 us -> 21 us  [kept_table(): pl.pallas_call(functools.partial(kernel, nlat, nrep, cols, trunc), out_sh...]
where the time goes in v4:
time: 22.5 us; the launch traced here: 22.4 us
  Pallas kernels  21 us (93%)
  local copies, waits for them, and re-layouts  1.33 us (6%)
    pallas_call x1, Pallas kernels, kept_table(): pl.pallas_call(functools.partial(kernel, nlat, nrep, cols, trunc), out_sh...  21 us
    unnamed x3, local copies, waits for them, and re-layouts  1.33 us

profile of v4, /device:TPU:0, one launch (start us, length us, event | category | flops | bytes accessed | tf_op | source)
XLA Modules:
  0.0 22.4 jit_solution(6259284267461312092)
XLA Ops:
  0.0 0.0 copy-start
  0.0 0.7 %copy-done = s32[4,8]{1,0:T(4,128)S(1)} copy-done((s32[4,8]{1,0:T(4,128)S(1)}, s32[4,8]{1,0:T(4,128)}, u32[]{:S(2)}) %copy-start) | copy-done | bytes 152
  0.7 21.0 %shard_map.37 = f32[4,6,1,1025]{3,2,1,0:T(1,128)S(1)} custom-call(s32[4,8]{1,0:T(4,128)S(1)} %copy-done, bf16[8200,128]{1,0:T(8,128)(2,1)} %bitcast.10, bf16[2,4,96,128]{3,2,1,0:T(8,128)(2,1)} %bitcast.11), custom_call_target="tpu_custom_call" | custom-call | flops 301989888 | bytes 2099200 | tf_op jit(solution)/shard_map/pallas_call | solution.py:281
  21.7 0.6 %copy.5 = f32[4,1,1025,6]{2,1,3,0:T(1,128)} copy(f32[4,1,1025,6]{2,1,3,0:T(1,128)S(1)} %bitcast.9) | data formatting | bytes 196800
Async XLA Ops:
  0.0 0.7 %copy-start = (s32[4,8]{1,0:T(4,128)S(1)}, s32[4,8]{1,0:T(4,128)}, u32[]{:S(2)}) copy-start(s32[4,8]{1,0:T(4,128)} %low_hbm.1) | copy-start | bytes 388
